TPU v7x, 32 devices: a whole 2x2x4 slice. The times are simulated.
32 devices in a mesh: dp: 4 (over z), tensor: 8 (over y, x, core).
Axes of the slice: x: 2, y: 2, z: 4, core: 2. Of those that a mesh axis runs over, the one named last changes fastest.
Arguments:
- activations: bfloat16 [3072, 4096], P('dp', 'tensor'), may hold values from -6 to 6
- out_grads_t: bfloat16 [5504, 3072], P('tensor', 'dp'), may hold values from -6 to 6
- in_basis: bfloat16 [4096, 4096], P(None, 'tensor'), may hold values from -0.09375 to 0.09375
- out_basis_t: bfloat16 [5504, 5504], P('tensor'), may hold values from -0.078125 to 0.078125
- query_proj: bfloat16 [4, 5504, 4096], P(None, 'tensor', 'dp'), may hold values from -6 to 6
- eigvals: float32 [5504, 4096], P('tensor', 'dp'), may hold values from 0.05 to 5
- damping: float32 [1], replicated, may hold values from 0.05 to 0.2
- lengths: int32 [24], P('dp'), may hold values from 1 to 128, 1920 in all
Outputs:
- scores: float32 [24, 4], P('dp')
Inputs may be any that keep to these rules, and one draw needn't show every extreme that they name: `lengths`: the largest token count is exactly 128.
All inputs are finite; a program needn't handle non-finite values. No bound on the sum of `lengths` on one device may be relied on, other than what follows from the above.
Results may differ from a plain program's by a relative error of at most 0.006.
Values may be sent and summed in bfloat16 or wider, within the bound.
A program may use at most 128 MiB of HBM per device.

v0:
```python
import jax
import jax.numpy as jnp
from jax import lax
from jax.sharding import PartitionSpec as P


def local(activations, out_grads_t, in_basis, out_basis_t, query_proj, eigvals, damping, lengths):
    full_act = lax.all_gather(activations, "tensor", axis=1, tiled=True)
    act_local = jnp.dot(full_act, in_basis, preferred_element_type=jnp.float32).astype(jnp.bfloat16)
    act_proj = lax.all_gather(act_local, "tensor", axis=1, tiled=True)
    token_rows = full_act.shape[0]
    width = out_basis_t.shape[0]
    grad_full = jnp.dot(
        out_basis_t,
        lax.all_gather(out_grads_t, "tensor", axis=0, tiled=True),
        preferred_element_type=jnp.float32,
    )
    seq_count = lengths.shape[0]
    seq_len = token_rows // seq_count
    position = lax.broadcasted_iota(jnp.int32, (seq_count, seq_len), 1)
    keep = (position < lengths[:, None]).astype(jnp.float32).reshape(1, token_rows)
    grad_proj = (grad_full * keep).astype(jnp.bfloat16)
    scaled = (query_proj.astype(jnp.float32) / (eigvals + damping[0])).astype(jnp.bfloat16)
    query_count = query_proj.shape[0]
    mixed = jnp.einsum(
        "td,qjd->qjt",
        act_proj,
        lax.all_gather(scaled, "dp", axis=2, tiled=True),
        preferred_element_type=jnp.float32,
    )
    weighted = mixed * grad_proj.astype(jnp.float32)[None, :, :]
    partial_value = jnp.sum(weighted.reshape(query_count, width, seq_count, seq_len), axis=(1, 3)).T
    totals = lax.psum(partial_value, "tensor")
    norm_factor = (act_proj.shape[1] * out_basis_t.shape[1] * seq_len) ** (-0.5)
    return totals * norm_factor


def solution(mesh):
    placed = (
        P("dp", "tensor"),
        P("tensor", "dp"),
        P(None, "tensor"),
        P("tensor", None),
        P(None, "tensor", "dp"),
        P("tensor", "dp"),
        P(),
        P("dp"),
    )
    return jax.shard_map(
        local, mesh=mesh, in_specs=placed, out_specs=P("dp", None), check_vma=False
    )
```

profile of v0, /device:TPU:0, one launch (start us, length us, event | category | flops | bytes accessed | tf_op | source)
XLA Modules:
  0.0 591.1 jit_solution(7677577895891891836)
XLA Ops:
  6.5 0.0 all-gather.7.cloned.1.call-start
  6.5 0.7 all-gather.7.cloned.1.call-update
  7.3 0.0 all-gather.11.cloned.1.call-start
  7.3 0.7 all-gather.11.cloned.1.call-update
  8.0 0.0 copy-start
  8.0 0.0 all-gather.9.cloned.1.call-start
  8.1 50.5 %all-gather.7.cloned.1.call-done = bf16[768,4096]{1,0:T(8,128)(2,1)} async-done(((bf16[768,512]{1,0:T(8,128)(2,1)}), bf16[768,4096]{1,0:T(8,128)(2,1)}) %all-gather.7.cloned.1.call-update) | async-done | bytes 6291472 | tf_op jit(solution)/shard_map/all_gather | solution.py:8
  58.5 8.3 %convolution_convert_fusion = bf16[768,512]{1,0:T(8,128)(2,1)} fusion(bf16[768,4096]{1,0:T(8,128)(2,1)} %all-gather.7.cloned.1.call-done, bf16[4096,512]{1,0:T(8,128)(2,1)} %param.10), kind=kOutput, calls=%fused_computation.7 | convolution fusion | flops 3221618688 | bytes 11272192 | tf_op jit(solution)/shard_map/dot_general | solution.py:9
  66.9 0.0 all-gather.9.cloned.1.call-update
  66.9 0.0 all-gather.5.cloned.1.call-start
  67.6 0.0 copy-done
  67.6 0.5 broadcast_add_fusion
  68.1 0.0 copy-start.1
  68.1 7.5 %divide_convert_fusion = bf16[4,688,1024]{2,1,0:T(8,128)(2,1)} fusion(bf16[4,688,1024]{2,1,0:T(8,128)(2,1)} %param.12, f32[688,1024]{1,0:T(8,128)S(1)} %broadcast_add_fusion), kind=kLoop, calls=%fused_computation | loop fusion | flops 8454144 | bytes 14090240 | tf_op jit(solution)/shard_map/convert_element_type | solution.py:23
  75.6 0.0 all-gather.5.cloned.1.call-update
  75.6 0.0 copy-done.1
  75.6 0.1 convert_bitcast_fusion
  75.7 39.3 %all-gather.11.cloned.1.call-done = bf16[5504,768]{1,0:T(8,128)(2,1)} async-done(((bf16[688,768]{1,0:T(8,128)(2,1)}), bf16[5504,768]{1,0:T(8,128)(2,1)}) %all-gather.11.cloned.1.call-update) | async-done | bytes 8454160 | tf_op jit(solution)/shard_map/all_gather | solution.py:15
  115.0 10.9 %fusion.4 = f32[688,768]{1,0:T(8,128)S(1)} fusion(bf16[688,5504]{1,0:T(8,128)(2,1)} %param.11, bf16[5504,768]{1,0:T(8,128)(2,1)} %all-gather.11.cloned.1.call-done, f32[768]{0:T(1024)S(1)} %convert_bitcast_fusion), kind=kOutput, calls=%fused_computation.5 | convolution fusion | flops 5818036224 | bytes 18144256 | tf_op jit(solution)/shard_map/dot_general | solution.py:13
  125.9 37.6 %all-gather.9.cloned.1.call-done = bf16[768,4096]{1,0:T(8,128)(2,1)} async-done(((bf16[768,512]{1,0:T(8,128)(2,1)}), bf16[768,4096]{1,0:T(8,128)(2,1)}) %all-gather.9.cloned.1.call-update) | async-done | bytes 6291472 | tf_op jit(solution)/shard_map/all_gather | solution.py:10
  163.5 384.0 %all-gather.5.cloned.1.call-done = bf16[4,688,4096]{2,1,0:T(8,128)(2,1)} async-done(((bf16[4,688,1024]{2,1,0:T(8,128)(2,1)}), bf16[4,688,4096]{2,1,0:T(8,128)(2,1)}) %all-gather.5.cloned.1.call-update) | async-done | bytes 22544400 | tf_op jit(solution)/shard_map/all_gather | solution.py:28
  547.5 22.8 %multiply_reduce_fusion = f32[4,768]{1,0:T(4,128)S(1)} fusion(f32[688,768]{1,0:T(8,128)S(1)} %fusion.4, bf16[4,688,4096]{2,1,0:T(8,128)(2,1)} %all-gather.5.cloned.1.call-done, bf16[768,4096]{1,0:T(8,128)(2,1)} %all-gather.9.cloned.1.call-done), kind=kOutput, calls=%fused_computation.1 | convolution fusion | flops 17318309888 | bytes 30961664 | tf_op jit(solution)/shard_map/td,qjd->qjt/dot_general | solution.py:25
  570.3 0.1 reduce_sum.18
  570.4 13.6 %psum.7 = f32[6,4]{0,1:T(4,128)S(1)} all-reduce(f32[6,4]{0,1:T(4,128)S(1)} %bitcast.15), channel_id=1, replica_groups=mesh['dp'=4,'tensor'=8] {'tensor'}, use_global_device_ids=true, to_apply=%region_2.3 | all-reduce | flops 24 | bytes 192 | tf_op jit(solution)/shard_map/psum | solution.py:33
  584.0 0.6 broadcast_multiply_fusion
  (1 shorter events, 0.0 us)
Async XLA Ops:
  6.5 52.0 %all-gather.7.cloned.1.call-start = ((), (), s32[]{:S(2)}) async-start(), calls=%async_computation.1 | async-start | bytes 7077888 | tf_op jit(solution)/shard_map/all_gather | solution.py:8
  7.3 107.7 %all-gather.11.cloned.1.call-start = ((), (), s32[]{:S(2)}) async-start(), calls=%async_computation.3 | async-start | bytes 9510912 | tf_op jit(solution)/shard_map/all_gather | solution.py:15
  8.0 59.6 %copy-start = (f32[688,1024]{1,0:T(8,128)S(1)}, f32[688,1024]{1,0:T(8,128)}, u32[]{:S(2)}) copy-start(f32[688,1024]{1,0:T(8,128)} %param.13) | copy-start | bytes 8454148
  8.0 155.5 %all-gather.9.cloned.1.call-start = ((), (), s32[]{:S(2)}) async-start(), calls=%async_computation.2 | async-start | bytes 7077888 | tf_op jit(solution)/shard_map/all_gather | solution.py:10
  66.9 480.6 %all-gather.5.cloned.1.call-start = ((), (), s32[]{:S(2)}) async-start(), calls=%async_computation | async-start | bytes 28180480 | tf_op jit(solution)/shard_map/all_gather | solution.py:28
  68.1 7.5 %copy-start.1 = (s32[6]{0:T(128)S(1)}, s32[6]{0:T(128)}, u32[]{:S(2)}) copy-start(s32[6]{0:T(128)} %param.15) | copy-start | bytes 76
Sparse Core Ops, SparseCore 0:
  9.2 49.2 all-gather.6
  60.4 54.5 all-gather.10
  116.9 46.5 all-gather.8
  164.9 382.4 all-gather.4
where the time goes:
time: 591 us
  waiting for transfers between devices  513 us (87%)
  matrix products  42 us (7%)
  between operations  13.8 us (2%)
  blocking collectives  13.6 us (2%)
  other arithmetic  8.66 us (1%)
    all_gather x1, waiting for transfers between devices, local(): lax.all_gather(scaled, 'dp', axis=2, tiled=True)  384 us
    all_gather x1, waiting for transfers between devices, local(): full_act = lax.all_gather(activations, 'tensor', axis=1, tiled=True)  50.5 us
    all_gather x1, waiting for transfers between devices, local(): lax.all_gather(out_grads_t, 'tensor', axis=0, tiled=True)  39.3 us
    all_gather x1, waiting for transfers between devices, local(): act_proj = lax.all_gather(act_local, 'tensor', axis=1, tiled=True)  37.6 us
    dot_general x1, matrix products, local(): jnp.einsum('td,qjd->qjt', act_proj, lax.all_gather(scaled, 'dp', axis=2,...  22.8 us
    psum x1, blocking collectives, local(): totals = lax.psum(partial_value, 'tensor')  13.6 us
  transfers between devices with their start and end apart: 4, of which 4 were waited for; matrix products, arithmetic and copies ran while one was open for 5% of the time, Pallas kernels for 0%

commit v1 on v0

v1 whole, which is shorter than its diff:
```python
import jax
import jax.numpy as jnp
from jax import lax
from jax.sharding import PartitionSpec as P


def local(activations, out_grads_t, in_basis, out_basis_t, query_proj, eigvals, damping, lengths):
    bf16, f32 = jnp.bfloat16, jnp.float32
    seq_count = lengths.shape[0]
    full_act = lax.all_gather(activations, "tensor", axis=1, tiled=True)
    token_rows = full_act.shape[0]
    seq_len = token_rows // seq_count
    act_local = jnp.dot(full_act, in_basis, preferred_element_type=f32).astype(bf16)
    act_full = lax.all_gather(act_local, "tensor", axis=1, tiled=True)
    features = act_full.shape[1]
    act_proj = lax.all_to_all(act_full, "dp", split_axis=1, concat_axis=0, tiled=True)
    grad_full = jnp.dot(
        out_basis_t, lax.all_gather(out_grads_t, "tensor", axis=0, tiled=True), preferred_element_type=f32
    )
    position = lax.broadcasted_iota(jnp.int32, (seq_count, seq_len), 1)
    keep = (position < lengths[:, None]).astype(f32).reshape(1, token_rows)
    grad_local = (grad_full * keep).astype(bf16)
    grad_proj = lax.all_gather(grad_local, "dp", axis=1, tiled=True)
    scaled = (query_proj.astype(f32) / (eigvals + damping[0])).astype(bf16)
    mixed = jnp.einsum("td,qjd->qjt", act_proj, scaled, preferred_element_type=f32)
    weighted = mixed * grad_proj.astype(f32)[None, :, :]
    query_count, width, tokens = weighted.shape
    partial_value = jnp.sum(weighted.reshape(query_count, width, tokens // seq_len, seq_len), axis=(1, 3)).T
    totals = lax.psum(partial_value, ("dp", "tensor"))
    mine = lax.dynamic_slice_in_dim(totals, lax.axis_index("dp") * seq_count, seq_count, 0)
    norm_factor = (features * out_basis_t.shape[1] * seq_len) ** (-0.5)
    return mine * norm_factor


def solution(mesh):
    placed = (
        P("dp", "tensor"),
        P("tensor", "dp"),
        P(None, "tensor"),
        P("tensor", None),
        P(None, "tensor", "dp"),
        P("tensor", "dp"),
        P(),
        P("dp"),
    )
    return jax.shard_map(
        local, mesh=mesh, in_specs=placed, out_specs=P("dp", None), check_vma=False
    )
```

time: 591 us -> 406 us (0.69)
  waiting for transfers between devices: 513 us -> 289 us
  blocking collectives: 13.6 us -> 38.4 us
  local copies, waits for them, and re-layouts: 0.02 us -> 6.33 us
    all_gather x2, waiting for transfers between devices: 422 us -> 192 us  [the longest x1 146 us: local(): grad_proj = lax.all_gather(grad_local, 'dp', axis=1, tiled=True)]
    psum x1, blocking collectives: 13.6 us -> 38.4 us  [local(): totals = lax.psum(partial_value, ('dp', 'tensor'))]
    all_to_all x0 -> x1, local copies, waits for them, and re-layouts: none -> 6.32 us  [local(): lax.all_to_all(act_full, 'dp', split_axis=1, concat_axis=0, tiled=True)]
  transfers between devices with their start and end apart: 4 -> 5, of which waited for: 4 -> 4; matrix products, arithmetic and copies ran while one was open for 5% -> 7% of each run, Pallas kernels for 0% -> 0%
where the time goes in v1:
time: 406 us; the launch traced here: 405 us
  waiting for transfers between devices  289 us (71%)
  matrix products  42.6 us (10%)
  blocking collectives  38.4 us (9%)
  between operations  13.8 us (3%)
  other arithmetic  9.29 us (2%)
  local copies, waits for them, and re-layouts  6.33 us (2%)
  starting transfers between devices  5.92 us (1%)
    all_gather x1, waiting for transfers between devices, local(): grad_proj = lax.all_gather(grad_local, 'dp', axis=1, tiled=True)  146 us
    all_gather x1, waiting for transfers between devices, local(): full_act = lax.all_gather(activations, 'tensor', axis=1, tiled=True)  51.2 us
    all_gather x1, waiting for transfers between devices, local(): act_full = lax.all_gather(act_local, 'tensor', axis=1, tiled=True)  46 us
    all_gather x1, waiting for transfers between devices, local(): lax.all_gather(out_grads_t, 'tensor', axis=0, tiled=True)  44.2 us
    psum x1, blocking collectives, local(): totals = lax.psum(partial_value, ('dp', 'tensor'))  38.4 us
    dot_general x1, matrix products, local(): jnp.einsum('td,qjd->qjt', act_proj, scaled, preferred_element_type=f32)  22.6 us
    dot_general x1, matrix products, local(): jnp.dot(out_basis_t, lax.all_gather(out_grads_t, 'tensor', axis=0, tiled=...  11.7 us
    dot_general x1, matrix products, local(): jnp.dot(full_act, in_basis, preferred_element_type=f32).astype(bf16)  8.3 us
  transfers between devices with their start and end apart: 5, of which 4 were waited for; matrix products, arithmetic and copies ran while one was open for 7% of the time, Pallas kernels for 0%

profile of v1, /device:TPU:0, one launch (start us, length us, event | category | flops | bytes accessed | tf_op | source)
XLA Modules:
  0.0 405.4 jit_solution(16750571598699061149)
XLA Ops:
  6.5 0.0 all-gather.5.cloned.1.call-start
  6.5 0.7 all-gather.5.cloned.1.call-update
  7.3 0.0 all-gather.7.cloned.1.call-start
  7.3 51.2 %all-gather.5.cloned.1.call-done = bf16[768,4096]{1,0:T(8,128)(2,1)} async-done(((bf16[768,512]{1,0:T(8,128)(2,1)}), bf16[768,4096]{1,0:T(8,128)(2,1)}) %all-gather.5.cloned.1.call-update) | async-done | bytes 6291472 | tf_op jit(solution)/shard_map/all_gather | solution.py:10
  58.5 8.3 %convolution_convert_fusion = bf16[768,512]{1,0:T(8,128)(2,1)} fusion(bf16[768,4096]{1,0:T(8,128)(2,1)} %all-gather.5.cloned.1.call-done, bf16[4096,512]{1,0:T(8,128)(2,1)} %param.10), kind=kOutput, calls=%fused_computation.6 | convolution fusion | flops 3221618688 | bytes 11272192 | tf_op jit(solution)/shard_map/dot_general | solution.py:13
  66.8 0.0 all-gather.7.cloned.1.call-update
  66.9 0.0 all-gather.9.cloned.1.call-start
  66.9 0.7 all-gather.9.cloned.1.call-update
  67.6 46.0 %all-gather.7.cloned.1.call-done = bf16[768,4096]{1,0:T(8,128)(2,1)} async-done(((bf16[768,512]{1,0:T(8,128)(2,1)}), bf16[768,4096]{1,0:T(8,128)(2,1)}) %all-gather.7.cloned.1.call-update) | async-done | bytes 6291472 | tf_op jit(solution)/shard_map/all_gather | solution.py:14
  113.6 6.3 %copy.16 = bf16[96,4,8,1024]{3,2,0,1:T(8,128)(2,1)} copy(bf16[96,4,8,1024]{3,2,1,0:T(8,128)(2,1)} %bitcast.23) | data formatting | bytes 12582912 | tf_op jit(solution)/shard_map/all_to_all | solution.py:16
  119.9 0.0 copy-start.2
  119.9 5.6 %all-to-all-start = ((bf16[768,4,1024]{2,0,1:T(8,128)(2,1)}), bf16[768,4,1024]{2,0,1:T(8,128)(2,1)}, u32[]{:S(2)}, u32[]{:S(2)}) async-start(bf16[768,4,1024]{2,0,1:T(8,128)(2,1)} %bitcast.22), calls=%async_computation | async-start | bytes 12582912 | tf_op jit(solution)/shard_map/all_to_all | solution.py:16
  125.5 0.2 all-gather.11.cloned.1.call-start
  125.8 0.0 copy-done.2
  125.8 0.1 convert_bitcast_fusion
  125.9 0.0 copy-start
  125.9 44.2 %all-gather.9.cloned.1.call-done = bf16[5504,768]{1,0:T(8,128)(2,1)} async-done(((bf16[688,768]{1,0:T(8,128)(2,1)}), bf16[5504,768]{1,0:T(8,128)(2,1)}) %all-gather.9.cloned.1.call-update) | async-done | bytes 8454160 | tf_op jit(solution)/shard_map/all_gather | solution.py:18
  170.1 11.7 %multiply_convert_fusion = bf16[688,768]{1,0:T(8,128)(2,1)} fusion(bf16[688,5504]{1,0:T(8,128)(2,1)} %param.11, bf16[5504,768]{1,0:T(8,128)(2,1)} %all-gather.9.cloned.1.call-done, f32[768]{0:T(1024)S(1)} %convert_bitcast_fusion), kind=kOutput, calls=%fused_computation.4 | convolution fusion | flops 5817507840 | bytes 17087488 | tf_op jit(solution)/shard_map/dot_general | solution.py:17
  181.8 0.0 all-gather.11.cloned.1.call-update
  182.4 0.0 copy-done
  182.4 1.9 broadcast_add_fusion
  184.3 0.0 copy-start.1
  184.3 146.2 %all-gather.11.cloned.1.call-done = bf16[688,3072]{1,0:T(8,128)(2,1)} async-done(((bf16[688,768]{1,0:T(8,128)(2,1)}), bf16[688,3072]{1,0:T(8,128)(2,1)}) %all-gather.11.cloned.1.call-update) | async-done | bytes 4227088 | tf_op jit(solution)/shard_map/all_gather | solution.py:23
  330.6 6.6 %convert_element_type.31 = f32[688,3072]{1,0:T(8,128)} convert(bf16[688,3072]{1,0:T(8,128)(2,1)} %all-gather.11.cloned.1.call-done) | non-fusion elementwise | flops 2113536 | bytes 12681216 | tf_op jit(solution)/shard_map/convert_element_type | solution.py:26
  337.1 0.0 all-to-all-done
  337.1 0.0 copy-done.1
  337.1 22.6 %multiply_reduce_fusion = f32[4,3072]{1,0:T(4,128)S(1)} fusion(f32[688,3072]{1,0:T(8,128)} %convert_element_type.31, bf16[3072,1024,1]{1,0,2:T(8,128)(2,1)} %bitcast.3, bf16[4,688,1024]{2,1,0:T(8,128)(2,1)} %param.12, f32[688,1024]{1,0:T(8,128)S(1)} %copy-done.1), kind=kOutput, calls=%fused_computation | convolution fusion | flops 17339437056 | bytes 23248896 | tf_op jit(solution)/shard_map/td,qjd->qjt/dot_general | solution.py:25
  359.8 0.1 bitcast_reduce_fusion
  359.8 38.4 %psum.7 = f32[24,4]{0,1:T(4,128)S(1)} all-reduce(f32[24,4]{0,1:T(4,128)S(1)} %bitcast.25), channel_id=1, replica_groups=mesh['dp'=4,'tensor'=8] {'dp','tensor'}, use_global_device_ids=true, to_apply=%region_2.3 | all-reduce | flops 96 | bytes 768 | tf_op jit(solution)/shard_map/psum | solution.py:29
  398.2 0.6 dynamic-slice_multiply_fusion
Async XLA Ops:
  6.5 52.0 %all-gather.5.cloned.1.call-start = ((), (), s32[]{:S(2)}) async-start(), calls=%async_computation.1 | async-start | bytes 7077888 | tf_op jit(solution)/shard_map/all_gather | solution.py:10
  7.3 106.3 %all-gather.7.cloned.1.call-start = ((), (), s32[]{:S(2)}) async-start(), calls=%async_computation.2 | async-start | bytes 7077888 | tf_op jit(solution)/shard_map/all_gather | solution.py:14
  66.9 103.2 %all-gather.9.cloned.1.call-start = ((), (), s32[]{:S(2)}) async-start(), calls=%async_computation.3 | async-start | bytes 9510912 | tf_op jit(solution)/shard_map/all_gather | solution.py:18
  119.9 5.9 %copy-start.2 = (s32[6]{0:T(128)S(1)}, s32[6]{0:T(128)}, u32[]{:S(2)}) copy-start(s32[6]{0:T(128)} %param.15) | copy-start | bytes 76
  119.9 217.2 %all-to-all-start = ((bf16[768,4,1024]{2,0,1:T(8,128)(2,1)}), bf16[768,4,1024]{2,0,1:T(8,128)(2,1)}, u32[]{:S(2)}, u32[]{:S(2)}) async-start(bf16[768,4,1024]{2,0,1:T(8,128)(2,1)} %bitcast.22), calls=%async_computation | async-start | bytes 12582912 | tf_op jit(solution)/shard_map/all_to_all | solution.py:16
  125.5 205.0 %all-gather.11.cloned.1.call-start = ((), (), s32[]{:S(2)}) async-start(), calls=%async_computation.4 | async-start | bytes 5283840 | tf_op jit(solution)/shard_map/all_gather | solution.py:23
  125.9 56.6 %copy-start = (f32[688,1024]{1,0:T(8,128)S(1)}, f32[688,1024]{1,0:T(8,128)}, u32[]{:S(2)}) copy-start(f32[688,1024]{1,0:T(8,128)} %param.13) | copy-start | bytes 8454148
  184.3 152.8 %copy-start.1 = (f32[688,1024]{1,0:T(8,128)S(1)}, f32[688,1024]{1,0:T(8,128)}, u32[]{:S(2)}) copy-start(f32[688,1024]{1,0:T(8,128)} %broadcast_add_fusion) | copy-start | bytes 8454148
Sparse Core Ops, SparseCore 0:
  9.2 49.2 all-gather.4
  67.0 46.5 all-gather.6
  115.5 54.5 all-gather.8
  181.9 148.6 all-gather.10

commit v2 on v1

--- a/solution.py
+++ b/solution.py
@@ -1,10 +1,14 @@
+import functools
+
 import jax
 import jax.numpy as jnp
 from jax import lax
+from jax.experimental import pallas as pl
+from jax.experimental.pallas import tpu as pltpu
 from jax.sharding import PartitionSpec as P
 
 
-def local(activations, out_grads_t, in_basis, out_basis_t, query_proj, eigvals, damping, lengths):
+def generic(activations, out_grads_t, in_basis, out_basis_t, query_proj, eigvals, damping, lengths):
     bf16, f32 = jnp.bfloat16, jnp.float32
     seq_count = lengths.shape[0]
     full_act = lax.all_gather(activations, "tensor", axis=1, tiled=True)
@@ -32,6 +36,472 @@
     return mine * norm_factor
 
 
+MESH = pl.DeviceIdType.MESH
+CHUNK = 256
+
+
+def kernel(
+    planes, seq_len, act_ref, og_ref, in_ref, out_ref, query_ref, eig_ref, keep_ref, damp_ref, res_ref,
+    og_all, act_all, in_b, out_b, scaled, eig, a_all, a_part, a_loc, a_acc, g_all, g_acc, csum, tiles, got_z, got_p,
+    load_sem, gs_send, gs_recv, up_send, up_recv, dn_send, dn_recv, xp_send, xp_recv, xz_send, xz_recv,
+    rz_send, rz_recv, rp_send, rp_recv,
+):
+    bf16, f32 = jnp.bfloat16, jnp.float32
+    z, j = lax.axis_index("dp"), lax.axis_index("tensor")
+    members = act_all.shape[0]
+    rows, feats = act_ref.shape
+    width, tokens = og_ref.shape
+    depth = out_b.shape[1]
+    queries, span = scaled.shape[0], scaled.shape[2]
+    part = rows // members
+    chunks = tokens // CHUNK
+    jx = j + 2 - 4 * lax.rem(j // 2, 2)
+    jy = j + 4 - 8 * (j // 4)
+    jd = jx + 4 - 8 * (j // 4)
+
+    def mate(k):
+        return k + 1 - 2 * lax.rem(k, 2)
+
+    jp = mate(j)
+
+    loads = [
+        pltpu.make_async_copy(og_ref, og_all.at[pl.ds(pl.multiple_of(j * width, 16), width), :], load_sem.at[0]),
+        pltpu.make_async_copy(act_ref, act_all.at[j], load_sem.at[1]),
+        pltpu.make_async_copy(query_ref, scaled, load_sem.at[2]),
+        pltpu.make_async_copy(eig_ref, eig, load_sem.at[3]),
+        pltpu.make_async_copy(out_ref, out_b, load_sem.at[4]),
+        pltpu.make_async_copy(in_ref, in_b, load_sem.at[5]),
+    ]
+    for load in loads:
+        load.start()
+
+    barrier = pltpu.get_barrier_semaphore()
+    for step in range(1, members):
+        pl.semaphore_signal(barrier, inc=1, device_id={"tensor": lax.rem(j + step, members)}, device_id_type=MESH)
+    for step in range(1, planes):
+        pl.semaphore_signal(barrier, inc=1, device_id={"dp": lax.rem(z + step, planes)}, device_id_type=MESH)
+    pl.semaphore_wait(barrier, members + planes - 2)
+
+    def og_view(k, h):
+        if h is None:
+            return og_all.at[pl.ds(pl.multiple_of(k * width, 16), width), :]
+        return og_all.at[pl.ds(pl.multiple_of(k * width, 16), width), pl.ds(h * (tokens // 2), tokens // 2)]
+
+    def act_view(k, h):
+        if h is None:
+            return act_all.at[k]
+        return act_all.at[k, pl.ds(h * (rows // 2), rows // 2), :]
+
+    def a_view(k, h):
+        at = pl.ds(pl.multiple_of(k * part, 16), part)
+        if h is None:
+            return a_all.at[:, at, :]
+        return a_all.at[pl.ds(h * (planes // 2), planes // 2), at, :]
+
+    class Gather:
+        def __init__(self, op, view, own):
+            self.op, self.view, self.own = op, view, own
+            self.plan = [
+                (j, 0, jx), (j, 1, jx), (jy, 1, jx),
+                (j, 1, jy), (j, 0, jy), (jx, 0, jy),
+                (j, None, jp), (jx, None, jp), (jy, None, jp), (jd, 0, jp), (jd, 1, jp),
+            ]
+            self.landed = [
+                (jx, 0), (jx, 1), (jd, 1),
+                (jy, 1), (jy, 0), (jd, 0),
+                (jp, None), (mate(jx), None), (mate(jy), None), (mate(jd), 0), (mate(jd), 1),
+            ]
+
+        def copy(self, slot):
+            block, half, target = self.plan[slot]
+            src = self.own(half) if slot in (0, 1, 3, 4, 6) else self.view(block, half)
+            return pltpu.make_async_remote_copy(
+                src_ref=src, dst_ref=self.view(block, half), send_sem=gs_send.at[self.op, slot],
+                recv_sem=gs_recv.at[self.op, slot], device_id={"tensor": target}, device_id_type=MESH,
+            )
+
+        def start(self, *slots):
+            for slot in slots:
+                self.copy(slot).start()
+
+        def arrive(self, *slots):
+            for slot in slots:
+                block, half = self.landed[slot]
+                view = self.view(block, half)
+                pltpu.make_async_remote_copy(
+                    src_ref=view, dst_ref=view, send_sem=gs_send.at[self.op, slot],
+                    recv_sem=gs_recv.at[self.op, slot], device_id={"tensor": jp}, device_id_type=MESH,
+                ).wait_recv()
+
+        def begin(self):
+            self.start(0, 3, 1, 4, 6)
+
+        def relay(self):
+            self.arrive(0)
+            self.start(5)
+            self.arrive(3)
+            self.start(2)
+
+        def share_near(self):
+            self.arrive(1)
+            self.start(7)
+            self.arrive(4)
+            self.start(8)
+
+        def share_far(self):
+            self.arrive(5)
+            self.start(9)
+            self.arrive(2)
+            self.start(10)
+
+        def drain(self):
+            for slot in range(len(self.plan)):
+                self.copy(slot).wait_send()
+
+    def half_of(ref, h, axis):
+        if h is None:
+            return ref
+        size = ref.shape[axis] // 2
+        return ref.at[pl.ds(h * size, size), :] if axis == 0 else ref.at[:, pl.ds(h * size, size)]
+
+    og = Gather(0, og_view, lambda h: half_of(og_ref, h, 1))
+    act = Gather(1, act_view, lambda h: half_of(act_ref, h, 0))
+    acts = Gather(2, a_view, lambda h: a_view(j, h))
+
+    og.begin()
+    csum[...] = jnp.zeros_like(csum)
+
+    loads[2].wait()
+    loads[3].wait()
+    step_rows = 16
+
+    def scale(i, carry):
+        at = pl.ds(pl.multiple_of(i * step_rows, step_rows), step_rows)
+        below = eig[at, :] + damp_ref[0]
+        for q in range(queries):
+            scaled[q, at, :] = (scaled[q, at, :].astype(f32) / below).astype(bf16)
+        return carry
+
+    lax.fori_loop(0, width // step_rows, scale, 0)
+
+    og.relay()
+    act.begin()
+    og.share_near()
+    og.share_far()
+    og.arrive(6, 7, 8, 9, 10)
+    loads[0].wait()
+    loads[4].wait()
+
+    def up(block, n):
+        return pltpu.make_async_remote_copy(
+            src_ref=g_all.at[block, n], dst_ref=g_all.at[block, n], send_sem=up_send.at[block, n],
+            recv_sem=up_recv.at[block, n], device_id={"dp": lax.rem(z + 1, planes)}, device_id_type=MESH,
+        )
+
+    def down(block, n):
+        return pltpu.make_async_remote_copy(
+            src_ref=g_all.at[block, n], dst_ref=g_all.at[block, n], send_sem=dn_send.at[block, n],
+            recv_sem=dn_recv.at[block, n], device_id={"dp": lax.rem(z + planes - 1, planes)}, device_id_type=MESH,
+        )
+
+    top, bottom = z == planes - 1, z == 0
+
+    def service(level, n):
+        @pl.when(z - level >= 0)
+        def _():
+            up(z - level, n).wait_recv()
+
+        @pl.when((z - level >= 0) & (z < planes - 1))
+        def _():
+            up(z - level, n).start()
+
+        @pl.when(z + level < planes)
+        def _():
+            down(z + level, n).wait_recv()
+
+        @pl.when((z + level < planes) & (z > 0))
+        def _():
+            down(z + level, n).start()
+
+    k_tile = 3 * CHUNK
+    k_full = depth // k_tile
+
+    def project(n, carry):
+        at = pl.ds(pl.multiple_of(n * CHUNK, CHUNK), CHUNK)
+        k_rest = depth - k_full * k_tile
+        if k_rest:
+            g_acc[...] = jnp.dot(
+                out_b[:, pl.ds(k_full * k_tile, k_rest)], og_all[pl.ds(k_full * k_tile, k_rest), at],
+                preferred_element_type=f32,
+            )
+        else:
+            g_acc[...] = jnp.zeros_like(g_acc)
+
+        def inner(k, c):
+            deep = pl.ds(pl.multiple_of(k * k_tile, k_tile), k_tile)
+            g_acc[...] += jnp.dot(out_b[:, deep], og_all[deep, at], preferred_element_type=f32)
+            return c
+
+        lax.fori_loop(0, k_full, inner, 0)
+        g_all[z, n] = (g_acc[...] * keep_ref[0:1, at]).astype(bf16)
+
+        @pl.when(z < planes - 1)
+        def _():
+            up(z, n).start()
+
+        @pl.when(z > 0)
+        def _():
+            down(z, n).start()
+
+        return carry
+
+    lax.fori_loop(0, chunks, project, 0)
+
+    a_acc[...] = jnp.zeros_like(a_acc)
+    loads[1].wait()
+    loads[5].wait()
+
+    def contract(first):
+        def body(i, carry):
+            k = first + i * (mate(first) - first)
+            deep = pl.ds(pl.multiple_of(k * feats, feats), feats)
+            a_acc[...] += jnp.dot(act_all[k], in_b[deep, :], preferred_element_type=f32)
+            return carry
+
+        lax.fori_loop(0, 2, body, 0)
+
+    act.relay()
+    act.arrive(6)
+    contract(j)
+    act.share_near()
+    service(1, 0)
+    act.arrive(7)
+    contract(jx)
+    act.arrive(8)
+    contract(jy)
+    act.share_far()
+    act.arrive(9, 10)
+    contract(jd)
+    a_loc[...] = a_acc[...].astype(bf16)
+
+    def spread(to):
+        return pltpu.make_async_remote_copy(
+            src_ref=a_loc.at[pl.ds(pl.multiple_of(to * part, 16), part), :],
+            dst_ref=a_part.at[j], send_sem=xp_send.at[to], recv_sem=xp_recv.at[j],
+            device_id={"tensor": to}, device_id_type=MESH,
+        )
+
+    def spread_from(k):
+        return pltpu.make_async_remote_copy(
+            src_ref=a_part.at[k], dst_ref=a_part.at[k], send_sem=xp_send.at[k], recv_sem=xp_recv.at[k],
+            device_id={"tensor": k}, device_id_type=MESH,
+        )
+
+    for step in range(1, members):
+        spread(lax.rem(j + step, members)).start()
+    a_part[j] = a_loc[pl.ds(pl.multiple_of(j * part, 16), part), :]
+    service(1, 1)
+    for step in range(1, members):
+        spread_from(lax.rem(j + step, members)).wait_recv()
+
+    mine = pl.ds(pl.multiple_of(j * part, 16), part)
+    group = span // a_part.shape[2]
+
+    def lift(to, g):
+        lane = pl.ds(g * a_part.shape[2], a_part.shape[2])
+        return pltpu.make_async_remote_copy(
+            src_ref=a_part.at[to * group + g], dst_ref=a_all.at[z, mine, lane], send_sem=xz_send.at[to, g],
+            recv_sem=xz_recv.at[z, g], device_id={"dp": to}, device_id_type=MESH,
+        )
+
+    def lift_from(k, g):
+        lane = pl.ds(g * a_part.shape[2], a_part.shape[2])
+        view = a_all.at[k, mine, lane]
+        return pltpu.make_async_remote_copy(
+            src_ref=view, dst_ref=view, send_sem=xz_send.at[k, g], recv_sem=xz_recv.at[k, g],
+            device_id={"dp": k}, device_id_type=MESH,
+        )
+
+    for step in range(1, planes):
+        for g in range(group):
+            lift(lax.rem(z + step, planes), g).start()
+    for g in range(group):
+        a_all[z, mine, pl.ds(g * a_part.shape[2], a_part.shape[2])] = a_part[z * group + g]
+    for n in range(2, chunks):
+        service(1, n)
+    for step in range(1, planes):
+        for g in range(group):
+            lift_from(lax.rem(z + step, planes), g).wait_recv()
+
+    acts.begin()
+    service(2, 0)
+    acts.relay()
+    acts.share_near()
+    for n in range(1, chunks):
+        service(2, n)
+    acts.share_far()
+    acts.arrive(6, 7, 8, 9, 10)
+
+    turn = 1 - 2 * (z // (planes // 2))
+    for s in range(planes):
+        block = lax.rem(z + s * turn + planes, planes)
+
+        def score(n, carry, s=s, block=block):
+            if s > 2:
+                service(s, n)
+            at = pl.ds(pl.multiple_of(n * CHUNK, CHUNK), CHUNK)
+            for q in range(queries):
+                mixed = lax.dot_general(
+                    scaled[q], a_all[block, at, :], (((1,), (1,)), ((), ())), preferred_element_type=f32
+                )
+                csum[block, n, pl.ds(q, 1), :] = jnp.sum(
+                    mixed * g_all[block, n].astype(f32), axis=0, keepdims=True
+                )
+            return carry
+
+        lax.fori_loop(0, chunks, score, 0)
+
+    per = res_ref.shape[1]
+    lane_at = lax.broadcasted_iota(jnp.int32, (8, per), 1)
+    each = CHUNK // seq_len
+    for b in range(planes):
+        tile = jnp.zeros((8, per), f32)
+        for n in range(chunks):
+            for h in range(each):
+                total = jnp.sum(csum[b, n, :, h * seq_len:(h + 1) * seq_len], axis=1, keepdims=True)
+                tile = tile + jnp.where(lane_at == n * each + h, total, 0.0)
+        tiles[b] = tile
+
+    def fold(to):
+        return pltpu.make_async_remote_copy(
+            src_ref=tiles.at[to], dst_ref=got_z.at[z], send_sem=rz_send.at[to], recv_sem=rz_recv.at[z],
+            device_id={"dp": to}, device_id_type=MESH,
+        )
+
+    def fold_from(k):
+        return pltpu.make_async_remote_copy(
+            src_ref=got_z.at[k], dst_ref=got_z.at[k], send_sem=rz_send.at[k], recv_sem=rz_recv.at[k],
+            device_id={"dp": k}, device_id_type=MESH,
+        )
+
+    for step in range(1, planes):
+        fold(lax.rem(z + step, planes)).start()
+    got_z[z] = tiles[z]
+    for step in range(1, planes):
+        fold_from(lax.rem(z + step, planes)).wait_recv()
+    total = got_z[0]
+    for b in range(1, planes):
+        total = total + got_z[b]
+    got_p[j] = total
+
+    def share(to):
+        return pltpu.make_async_remote_copy(
+            src_ref=got_p.at[j], dst_ref=got_p.at[j], send_sem=rp_send.at[to], recv_sem=rp_recv.at[j],
+            device_id={"tensor": to}, device_id_type=MESH,
+        )
+
+    def share_from(k):
+        return pltpu.make_async_remote_copy(
+            src_ref=got_p.at[k], dst_ref=got_p.at[k], send_sem=rp_send.at[k], recv_sem=rp_recv.at[k],
+            device_id={"tensor": k}, device_id_type=MESH,
+        )
+
+    for step in range(1, members):
+        share(lax.rem(j + step, members)).start()
+    for step in range(1, members):
+        share_from(lax.rem(j + step, members)).wait_recv()
+    total = got_p[0]
+    for k in range(1, members):
+        total = total + got_p[k]
+    res_ref[...] = total
+
+    og.drain()
+    act.drain()
+    acts.drain()
+    for level in range(planes):
+        for n in range(chunks):
+            @pl.when((z - level >= 0) & (z < planes - 1))
+            def _():
+                up(z - level, n).wait_send()
+
+            @pl.when((z + level < planes) & (z > 0))
+            def _():
+                down(z + level, n).wait_send()
+    for step in range(1, members):
+        to = lax.rem(j + step, members)
+        spread(to).wait_send()
+        share(to).wait_send()
+    for step in range(1, planes):
+        to = lax.rem(z + step, planes)
+        for g in range(group):
+            lift(to, g).wait_send()
+        fold(to).wait_send()
+
+
+def fits(planes, members, activations, out_grads_t, in_basis, query_proj, seq_count):
+    rows, feats = activations.shape
+    width, tokens = out_grads_t.shape
+    cols, span = in_basis.shape[1], query_proj.shape[2]
+    return (
+        members == 8 and planes % 2 == 0 and rows == tokens and rows % (16 * members) == 0
+        and feats % 128 == 0 and cols % 128 == 0 and span % cols == 0 and width % 16 == 0
+        and tokens % CHUNK == 0 and CHUNK % (rows // seq_count) == 0 and (rows // seq_count) % 128 == 0
+        and seq_count <= 128 and query_proj.shape[0] <= 8
+    )
+
+
+def local(planes, members, activations, out_grads_t, in_basis, out_basis_t, query_proj, eigvals, damping, lengths):
+    seq_count = lengths.shape[0]
+    if not fits(planes, members, activations, out_grads_t, in_basis, query_proj, seq_count):
+        return generic(activations, out_grads_t, in_basis, out_basis_t, query_proj, eigvals, damping, lengths)
+    bf16, f32 = jnp.bfloat16, jnp.float32
+    rows, feats = activations.shape
+    width, tokens = out_grads_t.shape
+    features, cols = in_basis.shape
+    depth = out_basis_t.shape[1]
+    queries, _, span = query_proj.shape
+    seq_len = rows // seq_count
+    part, chunks, group = rows // members, tokens // CHUNK, span // cols
+    position = lax.broadcasted_iota(jnp.int32, (seq_count, seq_len), 1)
+    keep = jnp.broadcast_to((position < lengths[:, None]).astype(f32).reshape(1, tokens), (8, tokens))
+    any_space = pl.BlockSpec(memory_space=pl.ANY)
+    vmem = pl.BlockSpec(memory_space=pltpu.VMEM)
+    dma = pltpu.SemaphoreType.DMA
+    res = pl.pallas_call(
+        functools.partial(kernel, planes, seq_len),
+        out_shape=jax.ShapeDtypeStruct((8, 128), f32),
+        in_specs=[any_space] * 6 + [vmem, pl.BlockSpec(memory_space=pltpu.SMEM)],
+        out_specs=vmem,
+        scratch_shapes=[
+            pltpu.VMEM((members * width, tokens), bf16),
+            pltpu.VMEM((members, rows, feats), bf16),
+            pltpu.VMEM((features, cols), bf16),
+            pltpu.VMEM((width, depth), bf16),
+            pltpu.VMEM((queries, width, span), bf16),
+            pltpu.VMEM((width, span), f32),
+            pltpu.VMEM((planes, rows, span), bf16),
+            pltpu.VMEM((members, part, cols), bf16),
+            pltpu.VMEM((rows, cols), bf16),
+            pltpu.VMEM((rows, cols), f32),
+            pltpu.VMEM((planes, chunks, width, CHUNK), bf16),
+            pltpu.VMEM((width, CHUNK), f32),
+            pltpu.VMEM((planes, chunks, 8, CHUNK), f32),
+            pltpu.VMEM((planes, 8, 128), f32),
+            pltpu.VMEM((planes, 8, 128), f32),
+            pltpu.VMEM((members, 8, 128), f32),
+            dma((6,)), dma((3, 11)), dma((3, 11)),
+            dma((planes, chunks)), dma((planes, chunks)), dma((planes, chunks)), dma((planes, chunks)),
+            dma((members,)), dma((members,)), dma((planes, group)), dma((planes, group)),
+            dma((planes,)), dma((planes,)), dma((members,)), dma((members,)),
+        ],
+        compiler_params=pltpu.CompilerParams(
+            collective_id=0, has_side_effects=True, vmem_limit_bytes=63 * 1024 * 1024
+        ),
+    )(activations, out_grads_t, in_basis, out_basis_t, query_proj, eigvals, keep, damping)
+    norm_factor = (features * depth * seq_len) ** (-0.5)
+    return res[:queries, :seq_count].T * norm_factor
+
+
 def solution(mesh):
     placed = (
         P("dp", "tensor"),
@@ -44,5 +514,5 @@
         P("dp"),
     )
     return jax.shard_map(
-        local, mesh=mesh, in_specs=placed, out_specs=P("dp", None), check_vma=False
+        functools.partial(local, mesh.shape["dp"], mesh.shape["tensor"]), mesh=mesh, in_specs=placed, out_specs=P("dp", None), check_vma=False
     )

time: 406 us -> 165 us (0.41)
  waiting for transfers between devices: 289 us -> 0 us
  Pallas kernels: 0 us -> 161 us
  matrix products: 42.6 us -> 0 us
  blocking collectives: 38.4 us -> 0 us
  between operations: 13.8 us -> 0.66 us
  other arithmetic: 9.29 us -> 1.98 us
  starting transfers between devices: 5.92 us -> 0 us
  local copies, waits for them, and re-layouts: 6.33 us -> 0.6 us
    all_gather x4 -> x0, waiting for transfers between devices: 288 us -> none  [the longest x1 146 us: local(): grad_proj = lax.all_gather(grad_local, 'dp', axis=1, tiled=True)]
    pallas_call x0 -> x1, Pallas kernels: none -> 161 us  [local(): pl.pallas_call(functools.partial(kernel, planes, seq_len), out_shape=jax....]
    dot_general x3 -> x0, matrix products: 42.6 us -> none  [the longest x1 22.6 us: local(): jnp.einsum('td,qjd->qjt', act_proj, scaled, preferred_element_type=f32)]
    psum x1 -> x0, blocking collectives: 38.4 us -> none  [local(): totals = lax.psum(partial_value, ('dp', 'tensor'))]
    all_to_all x1 -> x0, local copies, waits for them, and re-layouts: 6.32 us -> none  [local(): lax.all_to_all(act_full, 'dp', split_axis=1, concat_axis=0, tiled=True)]
    convert_element_type x2 -> x1, other arithmetic: 6.65 us -> 0.73 us  [local(): (position < lengths[:, None]).astype(f32).reshape(1, tokens)]
    all_to_all x1 -> x0, starting transfers between devices: 5.61 us -> none  [local(): lax.all_to_all(act_full, 'dp', split_axis=1, concat_axis=0, tiled=True)]
  transfers between devices with their start and end apart: 5 -> 0, of which waited for: 4 -> 0; matrix products, arithmetic and copies ran while one was open for 7% -> 0% of each run, Pallas kernels for 0% -> 0%
where the time goes in v2:
time: 165 us; the launch traced here: 164 us
  Pallas kernels  161 us (98%)
  other arithmetic  1.98 us (1%)
    pallas_call x1, Pallas kernels, local(): pl.pallas_call(functools.partial(kernel, planes, seq_len), out_shape=jax....  161 us

profile of v2, /device:TPU:0, one launch (start us, length us, event | category | flops | bytes accessed | tf_op | source)
XLA Modules:
  0.0 164.3 jit_solution(8782617328342335733)
XLA Ops:
  0.7 0.7 convert_bitcast_fusion
  1.4 0.6 broadcast_in_dim.2.keep_ref
  2.0 161.1 %shard_map.82 = f32[8,128]{1,0:T(8,128)} custom-call(bf16[768,512]{1,0:T(8,128)(2,1)} %act_ref.1, bf16[688,768]{1,0:T(8,128)(2,1)} %og_ref.1, bf16[4096,512]{1,0:T(8,128)(2,1)} %in_ref.1, bf16[688,5504]{1,0:T(8,128)(2,1)} %out_ref.1, bf16[4,688,1024]{2,1,0:T(8,128)(2,1)} %query_ref.1, f32[688,1024]{1,0:T(8,128)} %eig_ref.1, ...), custom_call_target="tpu_custom_call" | custom-call | tf_op jit(solution)/shard_map/pallas_call | solution.py:470
  163.1 1.3 multiply_bitcast_fusion

commit v3 on v2

--- a/solution.py
+++ b/solution.py
@@ -82,10 +82,20 @@
         pl.semaphore_signal(barrier, inc=1, device_id={"dp": lax.rem(z + step, planes)}, device_id_type=MESH)
     pl.semaphore_wait(barrier, members + planes - 2)
 
-    def og_view(k, h):
-        if h is None:
-            return og_all.at[pl.ds(pl.multiple_of(k * width, 16), width), :]
-        return og_all.at[pl.ds(pl.multiple_of(k * width, 16), width), pl.ds(h * (tokens // 2), tokens // 2)]
+    cut = (width // 2 + 15) // 16 * 16
+
+    def og_rows(h):
+        return (0, width) if h is None else ((0, cut), (cut, width - cut))[h]
+
+    def og_view(lanes):
+        def view(k, h):
+            first, size = og_rows(h)
+            return og_all.at[pl.ds(pl.multiple_of(k * width + first, 16), size), lanes]
+
+        return view
+
+    def og_own(lanes):
+        return lambda h: og_ref.at[pl.ds(*og_rows(h)), lanes]
 
     def act_view(k, h):
         if h is None:
@@ -133,6 +143,12 @@
                     recv_sem=gs_recv.at[self.op, slot], device_id={"tensor": jp}, device_id_type=MESH,
                 ).wait_recv()
 
+        def open(self):
+            self.start(0, 3, 6)
+
+        def extend(self):
+            self.start(1, 4)
+
         def begin(self):
             self.start(0, 3, 1, 4, 6)
 
@@ -158,14 +174,13 @@
             for slot in range(len(self.plan)):
                 self.copy(slot).wait_send()
 
-    def half_of(ref, h, axis):
-        if h is None:
-            return ref
-        size = ref.shape[axis] // 2
-        return ref.at[pl.ds(h * size, size), :] if axis == 0 else ref.at[:, pl.ds(h * size, size)]
-
-    og = Gather(0, og_view, lambda h: half_of(og_ref, h, 1))
-    act = Gather(1, act_view, lambda h: half_of(act_ref, h, 0))
+    def act_own(h):
+        return act_ref if h is None else act_ref.at[pl.ds(h * (rows // 2), rows // 2), :]
+
+    early, late = pl.ds(0, CHUNK), pl.ds(CHUNK, tokens - CHUNK)
+    og = Gather(0, og_view(early), og_own(early))
+    act = Gather(1, act_view, act_own)
+    more = Gather(3, og_view(late), og_own(late))
     acts = Gather(2, a_view, lambda h: a_view(j, h))
 
     og.begin()
@@ -255,7 +270,7 @@
 
         return carry
 
-    lax.fori_loop(0, chunks, project, 0)
+    project(0, 0)
 
     a_acc[...] = jnp.zeros_like(a_acc)
     loads[1].wait()
@@ -271,6 +286,7 @@
         lax.fori_loop(0, 2, body, 0)
 
     act.relay()
+    more.open()
     act.arrive(6)
     contract(j)
     act.share_near()
@@ -279,6 +295,7 @@
     contract(jx)
     act.arrive(8)
     contract(jy)
+    service(2, 0)
     act.share_far()
     act.arrive(9, 10)
     contract(jd)
@@ -300,7 +317,9 @@
     for step in range(1, members):
         spread(lax.rem(j + step, members)).start()
     a_part[j] = a_loc[pl.ds(pl.multiple_of(j * part, 16), part), :]
-    service(1, 1)
+    more.extend()
+    more.relay()
+    service(3, 0)
     for step in range(1, members):
         spread_from(lax.rem(j + step, members)).wait_recv()
 
@@ -327,39 +346,51 @@
             lift(lax.rem(z + step, planes), g).start()
     for g in range(group):
         a_all[z, mine, pl.ds(g * a_part.shape[2], a_part.shape[2])] = a_part[z * group + g]
-    for n in range(2, chunks):
-        service(1, n)
+    more.share_near()
+    more.share_far()
     for step in range(1, planes):
         for g in range(group):
             lift_from(lax.rem(z + step, planes), g).wait_recv()
-
     acts.begin()
-    service(2, 0)
+    more.arrive(6, 7, 8, 9, 10)
+    lax.fori_loop(1, chunks, project, 0)
     acts.relay()
+    for n in range(1, chunks):
+        service(1, n)
     acts.share_near()
-    for n in range(1, chunks):
-        service(2, n)
+    service(2, 1)
     acts.share_far()
     acts.arrive(6, 7, 8, 9, 10)
+    for level in range(4, planes):
+        service(level, 0)
 
     turn = 1 - 2 * (z // (planes // 2))
-    for s in range(planes):
+
+    def score(s, n):
         block = lax.rem(z + s * turn + planes, planes)
-
-        def score(n, carry, s=s, block=block):
-            if s > 2:
-                service(s, n)
-            at = pl.ds(pl.multiple_of(n * CHUNK, CHUNK), CHUNK)
-            for q in range(queries):
-                mixed = lax.dot_general(
-                    scaled[q], a_all[block, at, :], (((1,), (1,)), ((), ())), preferred_element_type=f32
-                )
-                csum[block, n, pl.ds(q, 1), :] = jnp.sum(
-                    mixed * g_all[block, n].astype(f32), axis=0, keepdims=True
-                )
+        at = pl.ds(pl.multiple_of(n * CHUNK, CHUNK), CHUNK)
+        for q in range(queries):
+            mixed = lax.dot_general(
+                scaled[q], a_all[block, at, :], (((1,), (1,)), ((), ())), preferred_element_type=f32
+            )
+            csum[block, n, pl.ds(q, 1), :] = jnp.sum(mixed * g_all[block, n].astype(f32), axis=0, keepdims=True)
+
+    def score_loop(lo, hi, n):
+        def body(s, carry):
+            score(s, n)
             return carry
 
-        lax.fori_loop(0, chunks, score, 0)
+        lax.fori_loop(lo, hi, body, 0)
+
+    score_loop(0, planes, 0)
+    for n in range(2, chunks):
+        service(2, n)
+    for n in range(1, chunks):
+        score_loop(0, min(3, planes), n)
+    for n in range(1, chunks):
+        for level in range(3, planes):
+            service(level, n)
+        score_loop(min(3, planes), planes, n)
 
     per = res_ref.shape[1]
     lane_at = lax.broadcasted_iota(jnp.int32, (8, per), 1)
@@ -416,6 +447,7 @@
     res_ref[...] = total
 
     og.drain()
+    more.drain()
     act.drain()
     acts.drain()
     for level in range(planes):
@@ -445,7 +477,7 @@
     return (
         members == 8 and planes % 2 == 0 and rows == tokens and rows % (16 * members) == 0
         and feats % 128 == 0 and cols % 128 == 0 and span % cols == 0 and width % 16 == 0
-        and tokens % CHUNK == 0 and CHUNK % (rows // seq_count) == 0 and (rows // seq_count) % 128 == 0
+        and tokens % CHUNK == 0 and tokens > CHUNK and width > 32 and CHUNK % (rows // seq_count) == 0 and (rows // seq_count) % 128 == 0
         and seq_count <= 128 and query_proj.shape[0] <= 8
     )
 
@@ -489,7 +521,7 @@
             pltpu.VMEM((planes, 8, 128), f32),
             pltpu.VMEM((planes, 8, 128), f32),
             pltpu.VMEM((members, 8, 128), f32),
-            dma((6,)), dma((3, 11)), dma((3, 11)),
+            dma((6,)), dma((4, 11)), dma((4, 11)),
             dma((planes, chunks)), dma((planes, chunks)), dma((planes, chunks)), dma((planes, chunks)),
             dma((members,)), dma((members,)), dma((planes, group)), dma((planes, group)),
             dma((planes,)), dma((planes,)), dma((members,)), dma((members,)),

time: 165 us -> 142 us (0.86)
  Pallas kernels: 161 us -> 138 us
    pallas_call x1, Pallas kernels: 161 us -> 138 us  [local(): pl.pallas_call(functools.partial(kernel, planes, seq_len), out_shape=jax....]
where the time goes in v3:
time: 142 us
  Pallas kernels  138 us (97%)
  other arithmetic  1.98 us (1%)
    pallas_call x1, Pallas kernels, local(): pl.pallas_call(functools.partial(kernel, planes, seq_len), out_shape=jax....  138 us

profile of v3, /device:TPU:0, one launch (start us, length us, event | category | flops | bytes accessed | tf_op | source)
XLA Modules:
  0.0 141.7 jit_solution(4030502715255078676)
XLA Ops:
  0.7 0.7 convert_bitcast_fusion
  1.4 0.6 broadcast_in_dim.2.keep_ref
  2.0 138.5 %shard_map.82 = f32[8,128]{1,0:T(8,128)} custom-call(bf16[768,512]{1,0:T(8,128)(2,1)} %act_ref.1, bf16[688,768]{1,0:T(8,128)(2,1)} %og_ref.1, bf16[4096,512]{1,0:T(8,128)(2,1)} %in_ref.1, bf16[688,5504]{1,0:T(8,128)(2,1)} %out_ref.1, bf16[4,688,1024]{2,1,0:T(8,128)(2,1)} %query_ref.1, f32[688,1024]{1,0:T(8,128)} %eig_ref.1, ...), custom_call_target="tpu_custom_call" | custom-call | tf_op jit(solution)/shard_map/pallas_call | solution.py:502
  140.5 1.3 multiply_bitcast_fusion

commit v4 on v3

--- a/solution.py
+++ b/solution.py
@@ -102,11 +102,22 @@
             return act_all.at[k]
         return act_all.at[k, pl.ds(h * (rows // 2), rows // 2), :]
 
-    def a_view(k, h):
-        at = pl.ds(pl.multiple_of(k * part, 16), part)
-        if h is None:
-            return a_all.at[:, at, :]
-        return a_all.at[pl.ds(h * (planes // 2), planes // 2), at, :]
+    half = planes // 2
+    side = z // half
+
+    def a_view(turn):
+        base = lax.rem(side + turn, 2) * half
+
+        def view(k, h):
+            at = pl.ds(pl.multiple_of(k * part, 16), part)
+            if h is None:
+                return a_all.at[pl.ds(base, half), at, :]
+            return a_all.at[pl.ds(base + h * (half // 2), half // 2), at, :]
+
+        return view
+
+    def a_own(turn):
+        return lambda h: a_view(turn)(j, h)
 
     class Gather:
         def __init__(self, op, view, own):
@@ -177,11 +188,10 @@
     def act_own(h):
         return act_ref if h is None else act_ref.at[pl.ds(h * (rows // 2), rows // 2), :]
 
-    early, late = pl.ds(0, CHUNK), pl.ds(CHUNK, tokens - CHUNK)
-    og = Gather(0, og_view(early), og_own(early))
+    lanes = [pl.ds(0, CHUNK), pl.ds(CHUNK, CHUNK), pl.ds(2 * CHUNK, tokens - 2 * CHUNK)]
+    og, next_og, more = [Gather(op, og_view(at), og_own(at)) for op, at in zip((0, 4, 3), lanes)]
     act = Gather(1, act_view, act_own)
-    more = Gather(3, og_view(late), og_own(late))
-    acts = Gather(2, a_view, lambda h: a_view(j, h))
+    near, far = [Gather(op, a_view(turn), a_own(turn)) for op, turn in ((2, 0), (5, 1))]
 
     og.begin()
     csum[...] = jnp.zeros_like(csum)
@@ -200,7 +210,7 @@
     lax.fori_loop(0, width // step_rows, scale, 0)
 
     og.relay()
-    act.begin()
+    next_og.begin()
     og.share_near()
     og.share_far()
     og.arrive(6, 7, 8, 9, 10)
@@ -271,6 +281,13 @@
         return carry
 
     project(0, 0)
+    next_og.relay()
+    act.begin()
+    next_og.share_near()
+    next_og.share_far()
+    next_og.arrive(6, 7, 8, 9, 10)
+    lax.fori_loop(1, 2, project, 0)
+    service(1, 0)
 
     a_acc[...] = jnp.zeros_like(a_acc)
     loads[1].wait()
@@ -289,13 +306,13 @@
     more.open()
     act.arrive(6)
     contract(j)
+    service(2, 0)
     act.share_near()
-    service(1, 0)
     act.arrive(7)
     contract(jx)
     act.arrive(8)
     contract(jy)
-    service(2, 0)
+    service(1, 1)
     act.share_far()
     act.arrive(9, 10)
     contract(jd)
@@ -318,8 +335,9 @@
         spread(lax.rem(j + step, members)).start()
     a_part[j] = a_loc[pl.ds(pl.multiple_of(j * part, 16), part), :]
     more.extend()
+    service(3, 0)
+    service(2, 1)
     more.relay()
-    service(3, 0)
     for step in range(1, members):
         spread_from(lax.rem(j + step, members)).wait_recv()
 
@@ -347,27 +365,30 @@
     for g in range(group):
         a_all[z, mine, pl.ds(g * a_part.shape[2], a_part.shape[2])] = a_part[z * group + g]
     more.share_near()
+    service(3, 1)
     more.share_far()
     for step in range(1, planes):
         for g in range(group):
             lift_from(lax.rem(z + step, planes), g).wait_recv()
-    acts.begin()
+    near.begin()
     more.arrive(6, 7, 8, 9, 10)
-    lax.fori_loop(1, chunks, project, 0)
-    acts.relay()
-    for n in range(1, chunks):
+    lax.fori_loop(2, chunks, project, 0)
+    near.relay()
+    far.begin()
+    near.share_near()
+    for n in range(2, chunks):
         service(1, n)
-    acts.share_near()
-    service(2, 1)
-    acts.share_far()
-    acts.arrive(6, 7, 8, 9, 10)
+    near.share_far()
+    near.arrive(6, 7, 8, 9, 10)
     for level in range(4, planes):
-        service(level, 0)
-
-    turn = 1 - 2 * (z // (planes // 2))
+        for n in range(2):
+            service(level, n)
 
     def score(s, n):
-        block = lax.rem(z + s * turn + planes, planes)
+        ahead = side * half + lax.rem(z - side * half + s, half)
+        other = s - half
+        across = (1 - side) * half + (1 - side) * other + side * (half - 1 - other)
+        block = ahead + (s // half) * (across - ahead)
         at = pl.ds(pl.multiple_of(n * CHUNK, CHUNK), CHUNK)
         for q in range(queries):
             mixed = lax.dot_general(
@@ -382,15 +403,23 @@
 
         lax.fori_loop(lo, hi, body, 0)
 
-    score_loop(0, planes, 0)
+    score_loop(0, half, 0)
+    far.relay()
+    score_loop(0, half, 1)
+    far.share_near()
     for n in range(2, chunks):
         service(2, n)
-    for n in range(1, chunks):
-        score_loop(0, min(3, planes), n)
-    for n in range(1, chunks):
-        for level in range(3, planes):
+    far.share_far()
+    for n in range(2, chunks):
+        score_loop(0, half, n)
+    far.arrive(6, 7, 8, 9, 10)
+    score_loop(half, planes, 0)
+    score_loop(half, planes, 1)
+    for level in range(3, planes):
+        for n in range(2, chunks):
             service(level, n)
-        score_loop(min(3, planes), planes, n)
+    for n in range(2, chunks):
+        score_loop(half, planes, n)
 
     per = res_ref.shape[1]
     lane_at = lax.broadcasted_iota(jnp.int32, (8, per), 1)
@@ -447,9 +476,11 @@
     res_ref[...] = total
 
     og.drain()
+    next_og.drain()
     more.drain()
     act.drain()
-    acts.drain()
+    near.drain()
+    far.drain()
     for level in range(planes):
         for n in range(chunks):
             @pl.when((z - level >= 0) & (z < planes - 1))
@@ -475,9 +506,9 @@
     width, tokens = out_grads_t.shape
     cols, span = in_basis.shape[1], query_proj.shape[2]
     return (
-        members == 8 and planes % 2 == 0 and rows == tokens and rows % (16 * members) == 0
+        members == 8 and planes == 4 and rows == tokens and rows % (16 * members) == 0
         and feats % 128 == 0 and cols % 128 == 0 and span % cols == 0 and width % 16 == 0
-        and tokens % CHUNK == 0 and tokens > CHUNK and width > 32 and CHUNK % (rows // seq_count) == 0 and (rows // seq_count) % 128 == 0
+        and tokens % CHUNK == 0 and tokens > 2 * CHUNK and width > 32 and CHUNK % (rows // seq_count) == 0 and (rows // seq_count) % 128 == 0
         and seq_count <= 128 and query_proj.shape[0] <= 8
     )
 
@@ -521,7 +552,7 @@
             pltpu.VMEM((planes, 8, 128), f32),
             pltpu.VMEM((planes, 8, 128), f32),
             pltpu.VMEM((members, 8, 128), f32),
-            dma((6,)), dma((4, 11)), dma((4, 11)),
+            dma((6,)), dma((6, 11)), dma((6, 11)),
             dma((planes, chunks)), dma((planes, chunks)), dma((planes, chunks)), dma((planes, chunks)),
             dma((members,)), dma((members,)), dma((planes, group)), dma((planes, group)),
             dma((planes,)), dma((planes,)), dma((members,)), dma((members,)),

time: 142 us -> 143 us (level)
  no operation moved by 1% of the time
where the time goes in v4:
time: 143 us
  Pallas kernels  139 us (97%)
  other arithmetic  1.98 us (1%)
    pallas_call x1, Pallas kernels, local(): pl.pallas_call(functools.partial(kernel, planes, seq_len), out_shape=jax....  139 us

profile of v4, /device:TPU:0, one launch (start us, length us, event | category | flops | bytes accessed | tf_op | source)
XLA Modules:
  0.0 142.5 jit_solution(3468546532713774810)
XLA Ops:
  0.7 0.7 convert_bitcast_fusion
  1.4 0.6 broadcast_in_dim.2.keep_ref
  2.0 139.3 %shard_map.82 = f32[8,128]{1,0:T(8,128)} custom-call(bf16[768,512]{1,0:T(8,128)(2,1)} %act_ref.1, bf16[688,768]{1,0:T(8,128)(2,1)} %og_ref.1, bf16[4096,512]{1,0:T(8,128)(2,1)} %in_ref.1, bf16[688,5504]{1,0:T(8,128)(2,1)} %out_ref.1, bf16[4,688,1024]{2,1,0:T(8,128)(2,1)} %query_ref.1, f32[688,1024]{1,0:T(8,128)} %eig_ref.1, ...), custom_call_target="tpu_custom_call" | custom-call | tf_op jit(solution)/shard_map/pallas_call | solution.py:533
  141.3 1.3 multiply_bitcast_fusion
